TPU v7x, 32 devices: a whole 2x2x4 slice. The times are simulated.
32 devices in a mesh: grp: 4 (over y, x), node: 8 (over z, core).
Axes of the slice: x: 2, y: 2, z: 4, core: 2. Of those that a mesh axis runs over, the one named last changes fastest.
Arguments:
- coefficients: float32 [8192, 1024], P(('grp', 'node')), may hold values from -6 to 6
- transfer: float32 [5, 8192, 512], P(None, ('grp', 'node')), may hold values from -0.3125 to 0.3125
- ranks: int32 [5, 32], P(None, ('grp', 'node')), may hold values from 128 to 256, as said below
Outputs:
- applied: float32 [8192, 1024], P(('grp', 'node'))
Inputs may be any that keep to these rules, and one draw needn't show every extreme that they name: `ranks`: in each level some block has rank exactly 256 and some block rank 256 // 2.
All inputs are finite; a program needn't handle non-finite values.
Results may differ from a plain program's by a relative error of at most 0.00011.
Values sent between devices are 32-bit elements; how exact they have to be, the bound alone decides.
A program may use at most 128 MiB of HBM per device.

v0:
```python
import jax
import jax.numpy as jnp
from jax import lax
from jax.sharding import PartitionSpec as P


def from_partner(x, axis, stride):
    return lax.ppermute(x, axis, [(i, i ^ 1 << stride) for i in range(lax.axis_size(axis))])


def apply_level(current, matrix, limit, upper_half, mover):
    width = current.shape[0]
    own_cols = lax.dynamic_slice_in_dim(matrix, upper_half * width, width, 1)
    first_term = jnp.dot(
        own_cols, current, precision=lax.Precision.HIGHEST, preferred_element_type=jnp.float32
    )
    partner = mover(current)
    other_cols = lax.dynamic_slice_in_dim(matrix, (1 - upper_half) * width, width, 1)
    mixed = first_term + jnp.dot(
        other_cols, partner, precision=lax.Precision.HIGHEST, preferred_element_type=jnp.float32
    )
    row_ids = jnp.arange(width, dtype=jnp.int32)
    return jnp.where((row_ids < limit)[:, None], mixed, jnp.zeros_like(mixed))


def per_device(coefficients, transfer, ranks):
    node_bits = lax.axis_size("node").bit_length() - 1
    group_bits = lax.axis_size("grp").bit_length() - 1
    node_place = lax.axis_index("node")
    group_place = lax.axis_index("grp")
    current = coefficients
    for level_bit in range(node_bits):

        def node_move(values, bit_number=level_bit):
            return from_partner(values, "node", bit_number)

        upper_half = node_place >> level_bit & 1
        current = apply_level(
            current, transfer[level_bit], ranks[level_bit, 0], upper_half, node_move
        )
    for level_bit in range(group_bits):

        def group_move(values, bit_number=level_bit):
            return from_partner(values, "grp", bit_number)

        level = node_bits + level_bit
        upper_half = group_place >> level_bit & 1
        current = apply_level(current, transfer[level], ranks[level, 0], upper_half, group_move)
    return current


def solution(mesh):
    return jax.shard_map(
        per_device,
        mesh=mesh,
        in_specs=(
            P(("grp", "node"), None),
            P(None, ("grp", "node"), None),
            P(None, ("grp", "node")),
        ),
        out_specs=P(("grp", "node"), None),
        check_vma=False,
    )
```

profile of v0, /device:TPU:0, one launch (start us, length us, event | category | flops | bytes accessed | tf_op | source)
XLA Modules:
  0.0 138.4 jit_solution(2158998799999387504)
XLA Ops:
  0.0 0.5 collective-permute-start
  0.5 1.5 %fusion.41 = (s32[1,1]{0,1:T(1,128)}, s32[1,1]{0,1:T(1,128)}, s32[1,1]{0,1:T(1,128)}, s32[1,1]{0,1:T(1,128)}, s32[1,1]{0,1:T(1,128)}) fusion(s32[5,1]{0,1:T(1,128)} %param.5), kind=kLoop, calls=%fused_computation.51 | loop fusion | bytes 40 | tf_op jit(solution)/shard_map/slice | solution.py:48
  2.0 0.6 iota_compare_fusion
  2.6 0.0 copy-start
  2.6 2.0 %fusion.40 = (f32[1,256,512]{2,1,0:T(8,128)S(1)}, f32[1,256,512]{2,1,0:T(8,128)S(1)}, f32[1,256,512]{2,1,0:T(8,128)S(1)}, f32[1,256,512]{2,1,0:T(8,128)S(1)}, f32[1,256,512]{2,1,0:T(8,128)S(1)}) fusion(f32[5,256,512]{2,1,0:T(8,128)} %param.4), kind=kLoop, calls=%fused_computation.50 | loop fusion | bytes 5242880 | tf_op jit(solution)/shard_map/slice | solution.py:48
  4.6 0.0 copy-done
  4.7 1.0 fusion.10
  5.7 0.0 collective-permute-done
  5.7 2.3 %fusion.4 = f32[256,1024]{1,0:T(8,128)S(1)} fusion(f32[256,1024]{1,0:T(8,128)S(1)} %fusion.10, f32[256,1024]{1,0:T(8,128)} %collective-permute-done, pred[256]{0:T(512)(128)(4,1)S(1)} %iota_compare_fusion, f32[1,256,512]{2,1,0:T(8,128)S(1)} %get-tuple-element.8, s32[]{:T(128)S(6)} %select_n.51), kind=kOutput, calls=%fused_computation.9 | convolution fusion | flops 805830656 | bytes 3408388 | tf_op jit(solution)/shard_map/dot_general | solution.py:19
  8.0 2.6 %collective-permute-start.1 = (f32[256,1024]{1,0:T(8,128)S(1)}, f32[256,1024]{1,0:T(8,128)}, u32[]{:S(2)}, u32[]{:S(2)}) collective-permute-start(f32[256,1024]{1,0:T(8,128)S(1)} %fusion.4), channel_id=1, source_target_pairs={{0,2},{1,3},{2,0},{3,1},{4,6},{5,7},{6,4},{7,5},{8,10},{9,11},{10,... | collective-permute-start | bytes 3145736 | tf_op jit(solution)/shard_map/ppermute | solution.py:8
  10.6 0.6 iota_compare_fusion.1
  11.2 1.0 fusion.12
  12.3 22.3 %collective-permute-done.1 = f32[256,1024]{1,0:T(8,128)} collective-permute-done((f32[256,1024]{1,0:T(8,128)S(1)}, f32[256,1024]{1,0:T(8,128)}, u32[]{:S(2)}, u32[]{:S(2)}) %collective-permute-start.1) | collective-permute-done | bytes 1048608 | tf_op jit(solution)/shard_map/ppermute | solution.py:8
  34.6 2.3 %fusion.3 = f32[256,1024]{1,0:T(8,128)S(1)} fusion(f32[256,1024]{1,0:T(8,128)S(1)} %fusion.12, f32[256,1024]{1,0:T(8,128)} %collective-permute-done.1, pred[256]{0:T(512)(128)(4,1)S(1)} %iota_compare_fusion.1, f32[1,256,512]{2,1,0:T(8,128)S(1)} %get-tuple-element.9, s32[]{:T(128)S(6)} %select_n.53), kind=kOutput, calls=%fused_computation.7 | convolution fusion | flops 805830656 | bytes 3408388 | tf_op jit(solution)/shard_map/dot_general | solution.py:19
  36.8 2.8 %collective-permute-start.2 = (f32[256,1024]{1,0:T(8,128)S(1)}, f32[256,1024]{1,0:T(8,128)}, u32[]{:S(2)}, u32[]{:S(2)}) collective-permute-start(f32[256,1024]{1,0:T(8,128)S(1)} %fusion.3), channel_id=1, source_target_pairs={{0,4},{1,5},{2,6},{3,7},{4,0},{5,1},{6,2},{7,3},{8,12},{9,13},{10,... | collective-permute-start | bytes 3145736 | tf_op jit(solution)/shard_map/ppermute | solution.py:8
  39.7 0.6 iota_compare_fusion.2
  40.3 1.0 fusion.14
  41.3 44.0 %collective-permute-done.2 = f32[256,1024]{1,0:T(8,128)} collective-permute-done((f32[256,1024]{1,0:T(8,128)S(1)}, f32[256,1024]{1,0:T(8,128)}, u32[]{:S(2)}, u32[]{:S(2)}) %collective-permute-start.2) | collective-permute-done | bytes 1048608 | tf_op jit(solution)/shard_map/ppermute | solution.py:8
  85.4 2.3 %fusion.2 = f32[256,1024]{1,0:T(8,128)S(1)} fusion(f32[256,1024]{1,0:T(8,128)S(1)} %fusion.14, f32[256,1024]{1,0:T(8,128)} %collective-permute-done.2, pred[256]{0:T(512)(128)(4,1)S(1)} %iota_compare_fusion.2, f32[1,256,512]{2,1,0:T(8,128)S(1)} %get-tuple-element.6, s32[]{:T(128)S(6)} %select_n.55), kind=kOutput, calls=%fused_computation.5 | convolution fusion | flops 805830656 | bytes 3408388 | tf_op jit(solution)/shard_map/dot_general | solution.py:19
  87.7 1.4 %collective-permute-start.3 = (f32[256,1024]{1,0:T(8,128)S(1)}, f32[256,1024]{1,0:T(8,128)S(1)}, u32[]{:S(2)}, u32[]{:S(2)}) collective-permute-start(f32[256,1024]{1,0:T(8,128)S(1)} %fusion.2), channel_id=1, source_target_pairs={{0,8},{8,0},{16,24},{24,16},{1,9},{9,1},{17,25},{25,17},{2,10},{10... | collective-permute-start | bytes 3145736 | tf_op jit(solution)/shard_map/ppermute | solution.py:8
  89.1 0.6 iota_compare_fusion.3
  89.7 1.0 fusion.16
  90.8 21.1 %collective-permute-done.3 = f32[256,1024]{1,0:T(8,128)S(1)} collective-permute-done((f32[256,1024]{1,0:T(8,128)S(1)}, f32[256,1024]{1,0:T(8,128)S(1)}, u32[]{:S(2)}, u32[]{:S(2)}) %collective-permute-start.3) | collective-permute-done | bytes 1048608 | tf_op jit(solution)/shard_map/ppermute | solution.py:8
  111.9 1.0 fusion.1
  113.0 1.3 collective-permute-start.4
  114.3 0.6 iota_compare_fusion.4
  115.0 1.0 fusion.18
  116.0 20.4 %collective-permute-done.4 = f32[256,1024]{1,0:T(8,128)S(1)} collective-permute-done((f32[256,1024]{1,0:T(8,128)S(1)}, f32[256,1024]{1,0:T(8,128)S(1)}, u32[]{:S(2)}, u32[]{:S(2)}) %collective-permute-start.4) | collective-permute-done | bytes 1048608 | tf_op jit(solution)/shard_map/ppermute | solution.py:8
  136.4 2.0 %fusion = f32[256,1024]{1,0:T(8,128)} fusion(f32[256,1024]{1,0:T(8,128)S(1)} %fusion.18, f32[256,1024]{1,0:T(8,128)S(1)} %collective-permute-done.4, pred[256]{0:T(512)(128)(4,1)S(1)} %iota_compare_fusion.4, f32[1,256,512]{2,1,0:T(8,128)S(1)} %get-tuple-element.5, s32[]{:T(128)S(6)} %select_n.59), kind=kOutput, calls=%fused_computation.1 | convolution fusion | flops 805830656 | bytes 3408388 | tf_op jit(solution)/shard_map/dot_general | solution.py:19
Async XLA Ops:
  0.0 5.7 %collective-permute-start = (f32[256,1024]{1,0:T(8,128)}, f32[256,1024]{1,0:T(8,128)}, u32[]{:S(2)}, u32[]{:S(2)}) collective-permute-start(f32[256,1024]{1,0:T(8,128)} %param.3), channel_id=1, source_target_pairs={{0,1},{1,0},{2,3},{3,2},{4,5},{5,4},{6,7},{7,6},{8,9},{9,8},{10,11... | collective-permute-start | bytes 3145736 | tf_op jit(solution)/shard_map/ppermute | solution.py:8
  2.6 2.0 %copy-start = (f32[256,1024]{1,0:T(8,128)S(1)}, f32[256,1024]{1,0:T(8,128)}, u32[]{:S(2)}) copy-start(f32[256,1024]{1,0:T(8,128)} %param.3) | copy-start | bytes 3145732
  8.0 26.6 %collective-permute-start.1 = (f32[256,1024]{1,0:T(8,128)S(1)}, f32[256,1024]{1,0:T(8,128)}, u32[]{:S(2)}, u32[]{:S(2)}) collective-permute-start(f32[256,1024]{1,0:T(8,128)S(1)} %fusion.4), channel_id=1, source_target_pairs={{0,2},{1,3},{2,0},{3,1},{4,6},{5,7},{6,4},{7,5},{8,10},{9,11},{10,... | collective-permute-start | bytes 3145736 | tf_op jit(solution)/shard_map/ppermute | solution.py:8
  36.8 48.5 %collective-permute-start.2 = (f32[256,1024]{1,0:T(8,128)S(1)}, f32[256,1024]{1,0:T(8,128)}, u32[]{:S(2)}, u32[]{:S(2)}) collective-permute-start(f32[256,1024]{1,0:T(8,128)S(1)} %fusion.3), channel_id=1, source_target_pairs={{0,4},{1,5},{2,6},{3,7},{4,0},{5,1},{6,2},{7,3},{8,12},{9,13},{10,... | collective-permute-start | bytes 3145736 | tf_op jit(solution)/shard_map/ppermute | solution.py:8
  87.7 24.3 %collective-permute-start.3 = (f32[256,1024]{1,0:T(8,128)S(1)}, f32[256,1024]{1,0:T(8,128)S(1)}, u32[]{:S(2)}, u32[]{:S(2)}) collective-permute-start(f32[256,1024]{1,0:T(8,128)S(1)} %fusion.2), channel_id=1, source_target_pairs={{0,8},{8,0},{16,24},{24,16},{1,9},{9,1},{17,25},{25,17},{2,10},{10... | collective-permute-start | bytes 3145736 | tf_op jit(solution)/shard_map/ppermute | solution.py:8
  113.0 23.4 %collective-permute-start.4 = (f32[256,1024]{1,0:T(8,128)S(1)}, f32[256,1024]{1,0:T(8,128)S(1)}, u32[]{:S(2)}, u32[]{:S(2)}) collective-permute-start(f32[256,1024]{1,0:T(8,128)S(1)} %fusion.1), channel_id=1, source_target_pairs={{0,16},{8,24},{16,0},{24,8},{1,17},{9,25},{17,1},{25,9},{2,18},{10... | collective-permute-start | bytes 3145736 | tf_op jit(solution)/shard_map/ppermute | solution.py:8
where the time goes:
time: 139 us; the launch traced here: 138 us
  waiting for transfers between devices  108 us (78%)
  matrix products  15.1 us (11%)
  starting transfers between devices  8.72 us (6%)
  local copies, waits for them, and re-layouts  3.49 us (3%)
  other arithmetic  3.14 us (2%)
    ppermute x5, waiting for transfers between devices, from_partner(): lax.ppermute(x, axis, [(i, i ^ 1 << stride) for i in range(lax.axis_size(...  108 us
    dot_general x5, matrix products, apply_level(): jnp.dot(other_cols, partner, precision=lax.Precision.HIGHEST, preferred_e...  9.89 us
    ppermute x5, starting transfers between devices, from_partner(): lax.ppermute(x, axis, [(i, i ^ 1 << stride) for i in range(lax.axis_size(...  8.72 us
    dot_general x5, matrix products, apply_level(): jnp.dot(own_cols, current, precision=lax.Precision.HIGHEST, preferred_ele...  5.18 us
    lt x5, other arithmetic, apply_level(): return jnp.where((row_ids < limit)[:, None], mixed, jnp.zeros_like(mixed))  3.14 us
  transfers between devices with their start and end apart: 5, of which 4 were waited for; matrix products, arithmetic and copies ran while one was open for 9% of the time, Pallas kernels for 0%

commit v1 on v0

v1 whole, which is shorter than its diff:
```python
import functools

import jax
import jax.numpy as jnp
from jax import lax
from jax.experimental import pallas as pl
from jax.experimental.pallas import tpu as pltpu
from jax.sharding import PartitionSpec as P

LANES = 128


def split_cols(x):
    high = x.astype(jnp.bfloat16)
    low = (x - high.astype(jnp.float32)).astype(jnp.bfloat16)
    return high, low


def plan(node_bits, group_bits):
    levels, due = [], 0
    for bit in range(node_bits):
        if bit:
            due += 1 if bit == 1 else 2
        levels.append(("node", bit, due))
    for bit in range(group_bits):
        due += 1
        levels.append(("grp", bit, due))
    return levels


def kernel(
    levels, ranks_ref, coef_ref, transfer_ref, out_ref,
    raw, mats, own, landed, mixed, stage,
    raw_sem, stage_sem, out_sem, send_sem, recv_sem,
):
    depth = coef_ref.shape[0]
    chunks, width = landed.shape[1], landed.shape[3]
    count = len(levels)

    places, partners = [], []
    for axis, bit, _ in levels:
        place = lax.axis_index(axis)
        upper = (place // 2**bit) % 2
        places.append(upper)
        partners.append({axis: place + (1 - 2 * upper) * 2**bit})

    def cols(chunk):
        return pl.ds(pl.multiple_of(chunk * width, width), width)

    def load_chunk(chunk):
        return pltpu.make_async_copy(
            coef_ref.at[:, cols(chunk)], stage.at[chunk], stage_sem.at[chunk]
        )

    def load_matrix(level):
        return pltpu.make_async_copy(transfer_ref.at[level], raw.at[level], raw_sem.at[level])

    def store_chunk(chunk):
        return pltpu.make_async_copy(
            mixed.at[count - 1, chunk], out_ref.at[:, cols(chunk)], out_sem.at[chunk]
        )

    def send(level, chunk):
        source = coef_ref.at[:, cols(chunk)] if level == 0 else mixed.at[level - 1, chunk]
        return pltpu.make_async_remote_copy(
            src_ref=source,
            dst_ref=landed.at[level, chunk],
            send_sem=send_sem.at[level, chunk],
            recv_sem=recv_sem.at[level, chunk],
            device_id=partners[level],
            device_id_type=pl.DeviceIdType.MESH,
        )

    barrier = pltpu.get_barrier_semaphore()
    for level in range(count):
        pl.semaphore_signal(
            barrier, inc=1, device_id=partners[level], device_id_type=pl.DeviceIdType.MESH
        )
    load_matrix(0).start()
    for chunk in range(chunks):
        load_chunk(chunk).start()
    for level in range(1, count):
        load_matrix(level).start()
    pl.semaphore_wait(barrier, count)
    for chunk in range(chunks):
        send(0, chunk).start()

    rows = lax.broadcasted_iota(jnp.int32, (depth, depth), 0)
    for level in range(count):
        load_matrix(level).wait()
        keep = rows < ranks_ref[0, level]
        for half, place in enumerate((places[level], 1 - places[level])):
            block = raw[level, :, pl.ds(pl.multiple_of(place * depth, depth), depth)]
            high, low = split_cols(jnp.where(keep, block, jnp.zeros_like(block)))
            mats[level, :depth, half * depth:(half + 1) * depth] = high
            mats[level, depth:, half * depth:(half + 1) * depth] = low

    def store_own(chunk, x):
        high, low = split_cols(x)
        own[chunk, :, :width] = high
        own[chunk, :, width:] = low

    for chunk in range(chunks):
        load_chunk(chunk).wait()
        store_own(chunk, stage[chunk])

    def task(level, chunk):
        send(level, chunk).wait_recv()
        other = jnp.concatenate(split_cols(landed[level, chunk]), axis=1)
        total = jnp.dot(
            mats[level, :, :depth], own[chunk], preferred_element_type=jnp.float32
        ) + jnp.dot(mats[level, :, depth:], other, preferred_element_type=jnp.float32)
        total = total[:depth] + total[depth:]
        result = total[:, :width] + total[:, width:]
        mixed[level, chunk] = result
        if level + 1 < count:
            store_own(chunk, result)
            send(level + 1, chunk).start()
        else:
            store_chunk(chunk).start()

    def step(s, carry):
        for level, (_, _, due) in enumerate(levels):
            @pl.when((s >= due) & (s < due + chunks))
            def _():
                task(level, s - due)
        return carry

    lax.fori_loop(0, levels[-1][2] + chunks, step, 0)

    def finish(chunk, carry):
        store_chunk(chunk).wait()
        for level in range(count):
            send(level, chunk).wait_send()
        return carry

    lax.fori_loop(0, chunks, finish, 0)


def per_device(coefficients, transfer, ranks):
    levels = plan(
        lax.axis_size("node").bit_length() - 1, lax.axis_size("grp").bit_length() - 1
    )
    count = len(levels)
    depth, width = coefficients.shape
    chunks = width // LANES
    call = pl.pallas_call(
        functools.partial(kernel, levels),
        out_shape=jax.ShapeDtypeStruct(coefficients.shape, jnp.float32),
        in_specs=[
            pl.BlockSpec(memory_space=pltpu.SMEM),
            pl.BlockSpec(memory_space=pl.ANY),
            pl.BlockSpec(memory_space=pl.ANY),
        ],
        out_specs=pl.BlockSpec(memory_space=pl.ANY),
        scratch_shapes=[
            pltpu.VMEM((count, depth, 2 * depth), jnp.float32),
            pltpu.VMEM((count, 2 * depth, 2 * depth), jnp.bfloat16),
            pltpu.VMEM((chunks, depth, 2 * LANES), jnp.bfloat16),
            pltpu.VMEM((count, chunks, depth, LANES), jnp.float32),
            pltpu.VMEM((count, chunks, depth, LANES), jnp.float32),
            pltpu.VMEM((chunks, depth, LANES), jnp.float32),
            pltpu.SemaphoreType.DMA((count,)),
            pltpu.SemaphoreType.DMA((chunks,)),
            pltpu.SemaphoreType.DMA((chunks,)),
            pltpu.SemaphoreType.DMA((count, chunks)),
            pltpu.SemaphoreType.DMA((count, chunks)),
        ],
        compiler_params=pltpu.CompilerParams(collective_id=0, has_side_effects=True),
        name="butterfly",
    )
    return call(ranks.T, coefficients, transfer)


def solution(mesh):
    return jax.shard_map(
        per_device,
        mesh=mesh,
        in_specs=(
            P(("grp", "node"), None),
            P(None, ("grp", "node"), None),
            P(None, ("grp", "node")),
        ),
        out_specs=P(("grp", "node"), None),
        check_vma=False,
    )
```

time: 139 us -> 73.8 us (0.53)
  waiting for transfers between devices: 108 us -> 0 us
  Pallas kernels: 0 us -> 71.3 us
  matrix products: 15.1 us -> 0 us
  starting transfers between devices: 8.72 us -> 0 us
  other arithmetic: 3.14 us -> 0 us
    ppermute x5 -> x0, waiting for transfers between devices: 108 us -> none  [from_partner(): lax.ppermute(x, axis, [(i, i ^ 1 << stride) for i in range(lax.axis_size(...]
    pallas_call x0 -> x1, Pallas kernels: none -> 71.3 us  [per_device(): return call(ranks.T, coefficients, transfer)]
    dot_general x10 -> x0, matrix products: 15.1 us -> none  [the longest x5 9.89 us: apply_level(): jnp.dot(other_cols, partner, precision=lax.Precision.HIGHEST, preferred_e...]
    ppermute x5 -> x0, starting transfers between devices: 8.72 us -> none  [from_partner(): lax.ppermute(x, axis, [(i, i ^ 1 << stride) for i in range(lax.axis_size(...]
    slice x2 -> x0, local copies, waits for them, and re-layouts: 3.49 us -> none  [the longest x1 2 us: per_device(): transfer[level]]
    lt x5 -> x0, other arithmetic: 3.14 us -> none  [apply_level(): return jnp.where((row_ids < limit)[:, None], mixed, jnp.zeros_like(mixed))]
    unnamed x2 -> x1, local copies, waits for them, and re-layouts: 0.01 us -> 2.31 us
  transfers between devices with their start and end apart: 5 -> 0, of which waited for: 4 -> 0; matrix products, arithmetic and copies ran while one was open for 9% -> 0% of each run, Pallas kernels for 0% -> 0%
where the time goes in v1:
time: 73.8 us; the launch traced here: 73.7 us
  Pallas kernels  71.3 us (97%)
  local copies, waits for them, and re-layouts  2.31 us (3%)
    pallas_call x1, Pallas kernels, per_device(): return call(ranks.T, coefficients, transfer)  71.3 us
    unnamed x1, local copies, waits for them, and re-layouts  2.31 us

profile of v1, /device:TPU:0, one launch (start us, length us, event | category | flops | bytes accessed | tf_op | source)
XLA Modules:
  0.0 73.7 jit_solution(562943347999150584)
XLA Ops:
  0.0 71.3 %butterfly.1 = f32[256,1024]{1,0:T(8,128)} custom-call(s32[1,5]{1,0:T(1,128)} %bitcast.1, f32[256,1024]{1,0:T(8,128)} %coef_ref.1, f32[5,256,512]{2,1,0:T(8,128)} %transfer_ref.1), custom_call_target="tpu_custom_call" | custom-call | tf_op jit(solution)/shard_map/butterfly/pallas_call | solution.py:172
  71.4 2.3 %copy.5 = f32[256,1024]{1,0:T(8,128)} copy(f32[256,1024]{1,0:T(8,128)} %butterfly.1) | data formatting | bytes 2097152

commit v2 on v1

v2 whole, which is shorter than its diff:
```python
import functools

import jax
import jax.numpy as jnp
from jax import lax
from jax.experimental import pallas as pl
from jax.experimental.pallas import tpu as pltpu
from jax.sharding import PartitionSpec as P

LANES = 128


def split_cols(x):
    high = x.astype(jnp.bfloat16)
    low = (x - high.astype(jnp.float32)).astype(jnp.bfloat16)
    return high, low


def plan(node_bits, group_bits):
    levels, due = [], 0
    for bit in range(node_bits):
        due += 3 if bit else 0
        levels.append(("node", bit, due))
    for bit in range(group_bits):
        due += 2
        levels.append(("grp", bit, due))
    return levels


def kernel(
    levels, ranks_ref, coef_ref, transfer_ref, out_ref,
    raw, mats, own_wide, own, first, landed, mixed, stage,
    raw_sem, stage_sem, first_send, first_recv, send_sem, recv_sem,
):
    depth = coef_ref.shape[0]
    chunks, _, width = first.shape
    pieces, short, _ = landed.shape[1:]
    half = width // 2
    count = len(levels)

    places, partners = [], []
    for axis, bit, _ in levels:
        place = lax.axis_index(axis)
        upper = (place // 2**bit) % 2
        places.append(upper)
        partners.append({axis: place + (1 - 2 * upper) * 2**bit})

    def cols(chunk):
        return pl.ds(pl.multiple_of(chunk * width, width), width)

    def load_chunk(chunk):
        return pltpu.make_async_copy(
            coef_ref.at[:, cols(chunk)], stage.at[chunk], stage_sem.at[chunk]
        )

    def load_matrix(level):
        return pltpu.make_async_copy(transfer_ref.at[level], raw.at[level], raw_sem.at[level])

    def send_first(chunk):
        return pltpu.make_async_remote_copy(
            src_ref=coef_ref.at[:, cols(chunk)],
            dst_ref=first.at[chunk],
            send_sem=first_send.at[chunk],
            recv_sem=first_recv.at[chunk],
            device_id=partners[0],
            device_id_type=pl.DeviceIdType.MESH,
        )

    def send(level, piece):
        return pltpu.make_async_remote_copy(
            src_ref=mixed.at[level - 1, piece],
            dst_ref=landed.at[level - 1, piece],
            send_sem=send_sem.at[level - 1, piece],
            recv_sem=recv_sem.at[level - 1, piece],
            device_id=partners[level],
            device_id_type=pl.DeviceIdType.MESH,
        )

    barrier = pltpu.get_barrier_semaphore()
    for level in range(count):
        pl.semaphore_signal(
            barrier, inc=1, device_id=partners[level], device_id_type=pl.DeviceIdType.MESH
        )
    load_matrix(0).start()
    for chunk in range(chunks):
        load_chunk(chunk).start()
    for level in range(1, count):
        load_matrix(level).start()
    pl.semaphore_wait(barrier, count)
    for chunk in range(chunks):
        send_first(chunk).start()

    left_lanes = lax.broadcasted_iota(jnp.int32, (short, width), 1) < half

    def turn(x):
        return pltpu.roll(x, half, 1)

    def prepare(level):
        load_matrix(level).wait()
        keep = lax.broadcasted_iota(jnp.int32, (depth, depth), 0) < ranks_ref[0, level]
        for side, place in enumerate((places[level], 1 - places[level])):
            block = raw[level, :, pl.ds(pl.multiple_of(place * depth, depth), depth)]
            high, low = split_cols(jnp.where(keep, block, jnp.zeros_like(block)))
            mats[level, :depth, side * depth:(side + 1) * depth] = high
            mats[level, depth:, side * depth:(side + 1) * depth] = low

    def mix(level, mine, other):
        total = jnp.dot(
            mats[level, :, :depth], mine, preferred_element_type=jnp.float32
        ) + jnp.dot(mats[level, :, depth:], other, preferred_element_type=jnp.float32)
        return total[:depth] + total[depth:]

    def spread(top, bottom):
        both = []
        for x in (top, bottom):
            high = x.astype(jnp.bfloat16).astype(jnp.float32)
            both.append(jnp.where(left_lanes, high, x - high).astype(jnp.bfloat16))
        return jnp.concatenate(both, axis=0)

    def spread_packed(packed):
        turned = turn(packed)
        top = jnp.where(left_lanes, packed, turned)
        bottom = jnp.where(left_lanes, turned, packed)
        return spread(top, bottom)

    def task_first(chunk):
        load_chunk(chunk).wait()
        own_wide[...] = jnp.concatenate(split_cols(stage[chunk]), axis=1)
        send_first(chunk).wait_recv()
        total = mix(0, own_wide[...], jnp.concatenate(split_cols(first[chunk]), axis=1))
        result = total[:, :width] + total[:, width:]
        top, bottom = result[:short], result[short:]
        packs = (
            jnp.where(left_lanes, top, turn(bottom)),
            jnp.where(left_lanes, turn(top), bottom),
        )
        for side, packed in enumerate(packs):
            piece = 2 * chunk + side
            mixed[0, piece] = packed
            own[piece] = spread_packed(packed)
            send(1, piece).start()

    def task(level, piece):
        send(level, piece).wait_recv()
        total = mix(level, own[piece], spread_packed(landed[level - 1, piece]))
        result = total + turn(total)
        if level + 1 < count:
            top, bottom = result[:short], result[short:]
            mixed[level, piece] = jnp.where(left_lanes, top, bottom)
            own[piece] = spread(top, bottom)
            send(level + 1, piece).start()
        else:
            here = cols(piece // 2)
            lanes = lax.broadcasted_iota(jnp.int32, (depth, width), 1)
            out_ref[:, here] = jnp.where(lanes < half * (piece % 2), out_ref[:, here], result)

    prepare(0)

    def step(s, carry):
        @pl.when((s % 2 == 0) & (s < pieces))
        def _():
            task_first(s // 2)

        for level, (_, _, due) in enumerate(levels):
            if level:
                @pl.when((s >= due) & (s < due + pieces))
                def _():
                    task(level, s - due)

            if level + 1 < count:
                @pl.when(s == due)
                def _():
                    prepare(level + 1)
        return carry

    lax.fori_loop(0, levels[-1][2] + pieces, step, 0)

    def finish(piece, carry):
        for level in range(1, count):
            send(level, piece).wait_send()
        return carry

    lax.fori_loop(0, pieces, finish, 0)

    def finish_first(chunk, carry):
        send_first(chunk).wait_send()
        return carry

    lax.fori_loop(0, chunks, finish_first, 0)


def per_device(coefficients, transfer, ranks):
    levels = plan(
        lax.axis_size("node").bit_length() - 1, lax.axis_size("grp").bit_length() - 1
    )
    count = len(levels)
    depth, width = coefficients.shape
    chunks = width // LANES
    pieces = 2 * chunks
    short = depth // 2
    call = pl.pallas_call(
        functools.partial(kernel, levels),
        out_shape=jax.ShapeDtypeStruct(coefficients.shape, jnp.float32),
        in_specs=[
            pl.BlockSpec(memory_space=pltpu.SMEM),
            pl.BlockSpec(memory_space=pltpu.HBM),
            pl.BlockSpec(memory_space=pltpu.HBM),
        ],
        out_specs=pl.BlockSpec(memory_space=pltpu.VMEM),
        scratch_shapes=[
            pltpu.VMEM((count, depth, 2 * depth), jnp.float32),
            pltpu.VMEM((count, 2 * depth, 2 * depth), jnp.bfloat16),
            pltpu.VMEM((depth, 2 * LANES), jnp.bfloat16),
            pltpu.VMEM((pieces, depth, LANES), jnp.bfloat16),
            pltpu.VMEM((chunks, depth, LANES), jnp.float32),
            pltpu.VMEM((count - 1, pieces, short, LANES), jnp.float32),
            pltpu.VMEM((count - 1, pieces, short, LANES), jnp.float32),
            pltpu.VMEM((chunks, depth, LANES), jnp.float32),
            pltpu.SemaphoreType.DMA((count,)),
            pltpu.SemaphoreType.DMA((chunks,)),
            pltpu.SemaphoreType.DMA((chunks,)),
            pltpu.SemaphoreType.DMA((chunks,)),
            pltpu.SemaphoreType.DMA((count - 1, pieces)),
            pltpu.SemaphoreType.DMA((count - 1, pieces)),
        ],
        compiler_params=pltpu.CompilerParams(
            collective_id=0, has_side_effects=True, vmem_limit_bytes=55_000_000
        ),
        name="butterfly",
    )
    return call(ranks.T, coefficients, transfer)


def solution(mesh):
    return jax.shard_map(
        per_device,
        mesh=mesh,
        in_specs=(
            P(("grp", "node"), None),
            P(None, ("grp", "node"), None),
            P(None, ("grp", "node")),
        ),
        out_specs=P(("grp", "node"), None),
        check_vma=False,
    )
```

time: 73.8 us -> 70.8 us (0.959)
  Pallas kernels: 71.3 us -> 69 us
    pallas_call x1, Pallas kernels: 71.3 us -> 69 us  [per_device(): return call(ranks.T, coefficients, transfer)]
    unnamed x1 -> x3, local copies, waits for them, and re-layouts: 2.31 us -> 1.63 us
where the time goes in v2:
time: 70.8 us; the launch traced here: 70.6 us
  Pallas kernels  69 us (97%)
  local copies, waits for them, and re-layouts  1.63 us (2%)
    pallas_call x1, Pallas kernels, per_device(): return call(ranks.T, coefficients, transfer)  69 us
    unnamed x3, local copies, waits for them, and re-layouts  1.63 us

profile of v2, /device:TPU:0, one launch (start us, length us, event | category | flops | bytes accessed | tf_op | source)
XLA Modules:
  0.0 70.6 jit_solution(2417196065949195804)
XLA Ops:
  0.0 0.0 copy-start
  0.0 0.7 copy-done
  0.7 69.0 %butterfly.1 = f32[256,1024]{1,0:T(8,128)S(1)} custom-call(s32[1,5]{1,0:T(1,128)S(1)} %bitcast.1, f32[256,1024]{1,0:T(8,128)} %coef_ref.1, f32[5,256,512]{2,1,0:T(8,128)} %transfer_ref.1), custom_call_target="tpu_custom_call" | custom-call | tf_op jit(solution)/shard_map/butterfly/pallas_call | solution.py:231
  69.7 1.0 %copy.5 = f32[256,1024]{1,0:T(8,128)} copy(f32[256,1024]{1,0:T(8,128)S(1)} %butterfly.1) | data formatting | bytes 2097152
Async XLA Ops:
  0.0 0.7 copy-start

commit v3 on v2

--- a/solution.py
+++ b/solution.py
@@ -19,7 +19,7 @@
 def plan(node_bits, group_bits):
     levels, due = [], 0
     for bit in range(node_bits):
-        due += 3 if bit else 0
+        due += (0, 2, 4)[min(bit, 2)]
         levels.append(("node", bit, due))
     for bit in range(group_bits):
         due += 2
@@ -29,7 +29,7 @@
 
 def kernel(
     levels, ranks_ref, coef_ref, transfer_ref, out_ref,
-    raw, mats, own_wide, own, first, landed, mixed, stage,
+    raw, mats, own, first, landed, mixed, stage,
     raw_sem, stage_sem, first_send, first_recv, send_sem, recv_sem,
 ):
     depth = coef_ref.shape[0]
@@ -104,11 +104,14 @@
             mats[level, :depth, side * depth:(side + 1) * depth] = high
             mats[level, depth:, side * depth:(side + 1) * depth] = low
 
-    def mix(level, mine, other):
-        total = jnp.dot(
-            mats[level, :, :depth], mine, preferred_element_type=jnp.float32
-        ) + jnp.dot(mats[level, :, depth:], other, preferred_element_type=jnp.float32)
+    def fold(total):
         return total[:depth] + total[depth:]
+
+    def mix_own(level, x):
+        return fold(jnp.dot(mats[level, :, :depth], x, preferred_element_type=jnp.float32))
+
+    def mix_other(level, x):
+        return fold(jnp.dot(mats[level, :, depth:], x, preferred_element_type=jnp.float32))
 
     def spread(top, bottom):
         both = []
@@ -125,9 +128,9 @@
 
     def task_first(chunk):
         load_chunk(chunk).wait()
-        own_wide[...] = jnp.concatenate(split_cols(stage[chunk]), axis=1)
+        mine = mix_own(0, jnp.concatenate(split_cols(stage[chunk]), axis=1))
         send_first(chunk).wait_recv()
-        total = mix(0, own_wide[...], jnp.concatenate(split_cols(first[chunk]), axis=1))
+        total = mine + mix_other(0, jnp.concatenate(split_cols(first[chunk]), axis=1))
         result = total[:, :width] + total[:, width:]
         top, bottom = result[:short], result[short:]
         packs = (
@@ -141,8 +144,9 @@
             send(1, piece).start()
 
     def task(level, piece):
+        mine = mix_own(level, own[piece])
         send(level, piece).wait_recv()
-        total = mix(level, own[piece], spread_packed(landed[level - 1, piece]))
+        total = mine + mix_other(level, spread_packed(landed[level - 1, piece]))
         result = total + turn(total)
         if level + 1 < count:
             top, bottom = result[:short], result[short:]
@@ -210,7 +214,6 @@
         scratch_shapes=[
             pltpu.VMEM((count, depth, 2 * depth), jnp.float32),
             pltpu.VMEM((count, 2 * depth, 2 * depth), jnp.bfloat16),
-            pltpu.VMEM((depth, 2 * LANES), jnp.bfloat16),
             pltpu.VMEM((pieces, depth, LANES), jnp.bfloat16),
             pltpu.VMEM((chunks, depth, LANES), jnp.float32),
             pltpu.VMEM((count - 1, pieces, short, LANES), jnp.float32),
@@ -228,7 +231,8 @@
         ),
         name="butterfly",
     )
-    return call(ranks.T, coefficients, transfer)
+    operands = (ranks.T, coefficients, transfer)
+    return call(*(pltpu.with_memory_space_constraint(x, pltpu.HBM) for x in operands))
 
 
 def solution(mesh):

time: 70.8 us -> 75 us (1.059)
  Pallas kernels: 69 us -> 73.9 us
    pallas_call x1, Pallas kernels: 69 us -> 73.9 us  [per_device(): call(*(pltpu.with_memory_space_constraint(x, pltpu.HBM) for x in operands))]
    unnamed x3 -> x1, local copies, waits for them, and re-layouts: 1.63 us -> 0.97 us
where the time goes in v3:
time: 75 us; the launch traced here: 74.9 us
  Pallas kernels  73.9 us (99%)
  local copies, waits for them, and re-layouts  0.97 us (1%)
    pallas_call x1, Pallas kernels, per_device(): call(*(pltpu.with_memory_space_constraint(x, pltpu.HBM) for x in operands))  73.9 us

profile of v3, /device:TPU:0, one launch (start us, length us, event | category | flops | bytes accessed | tf_op | source)
XLA Modules:
  0.0 74.9 jit_solution(4823328685371566463)
XLA Ops:
  0.0 73.9 %butterfly.1 = f32[256,1024]{1,0:T(8,128)S(1)} custom-call(s32[1,5]{1,0:T(1,128)} %bitcast.1, f32[256,1024]{1,0:T(8,128)} %coef_ref.1, f32[5,256,512]{2,1,0:T(8,128)} %transfer_ref.1), custom_call_target="tpu_custom_call" | custom-call | tf_op jit(solution)/shard_map/butterfly/pallas_call | solution.py:235
  73.9 1.0 %copy.5 = f32[256,1024]{1,0:T(8,128)} copy(f32[256,1024]{1,0:T(8,128)S(1)} %butterfly.1) | data formatting | bytes 2097152
